TPU v7x, 32 devices: a whole 2x2x4 slice. The times are simulated.
32 devices in a mesh: table: 16 (over z, y, x), ctx: 2 (over core).
Axes of the slice: x: 2, y: 2, z: 4, core: 2. Of those that a mesh axis runs over, the one named last changes fastest.
Arguments:
- item_table: float32 [32768, 256], P('table'), may hold values from -3 to 3
- serve_rows: int32 [256, 512], P('table', 'ctx'), may hold values from 0 to 2047, as said below
- token_slots: int32 [16, 2048, 4], P('table', 'ctx'), may hold values from 0 to 4095
- lengths: int32 [16], P('table'), may hold values from 1 to 2048, as said below
- w_proj: bfloat16 [256, 2048], replicated, may hold values from -0.375 to 0.375
- w_out: bfloat16 [512, 256], replicated, may hold values from -0.25 to 0.25
- grad_out: bfloat16 [16, 2048, 256], P('table', 'ctx'), may hold values from -6 to 6
Outputs:
- layer_out: bfloat16 [16, 2048, 256], P('table', 'ctx')
- grad_table: float32 [32768, 256], P(('table', 'ctx'))
Inputs may be any that keep to these rules, and one draw needn't show every extreme that they name: `serve_rows`: the 256 rows that one owner serves to one requesting device are distinct. `lengths`: some history has all 2048 actions.
All inputs are finite; a program needn't handle non-finite values.
Results may differ from a plain program's by a relative error of at most 0.009.
Values may be sent and summed in bfloat16 or wider, within the bound.
No kernel may reach another device: no remote copies, remote signals or barrier semaphores. Data moves between devices by JAX's collectives and lax.ppermute only.
A program may use at most 192 MiB of HBM per device.

v0:
```python
import jax
import jax.numpy as jnp
from jax import lax
from jax.sharding import PartitionSpec as P

HEAD = 128
epsilon = 1e-05
block_rows = 512


def silu_slope(inputs):
    sigmoid_value = jax.nn.sigmoid(inputs)
    return sigmoid_value * (1.0 + inputs * (1.0 - sigmoid_value))


def normalize(inputs):
    centred = inputs - jnp.mean(inputs, axis=-1, keepdims=True)
    inverse = lax.rsqrt(jnp.mean(centred * centred, axis=-1, keepdims=True) + epsilon)
    return (centred * inverse, inverse)


def norm_back(gradients, normed, inverse):
    return (
        gradients
        - jnp.mean(gradients, axis=-1, keepdims=True)
        - normed * jnp.mean(gradients * normed, axis=-1, keepdims=True)
    ) * inverse


def blockwise(step_fn, carried, pieces, first_row):
    row_total = pieces[0].shape[0]

    def visit_block(step_index, current):
        offset = step_index * block_rows
        subset = tuple(
            (lax.dynamic_slice_in_dim(one_piece, offset, block_rows, 0) for one_piece in pieces)
        )
        return step_fn(current, subset, first_row + offset)

    return lax.fori_loop(0, row_total // block_rows, visit_block, carried)


def split_heads(matrix):
    return matrix.reshape(matrix.shape[0], -1, HEAD)


def scores(query_rows, key_rows):
    return jnp.einsum(
        "ihd,jhd->hij",
        split_heads(query_rows),
        split_heads(key_rows),
        preferred_element_type=jnp.float32,
    ) * HEAD ** (-0.5)


def on_device(item_table, serve_rows, token_slots, lengths, w_proj, w_out, grad_out):
    row_width = item_table.shape[1]
    served = item_table[serve_rows]
    fetched = lax.all_to_all(served, "table", split_axis=0, concat_axis=0, tiled=True)
    fetched_rows = fetched.reshape(-1, row_width)
    slot_ids = token_slots[0]
    embedded = fetched_rows[slot_ids[:, 0]]
    for feature in range(1, slot_ids.shape[1]):
        embedded = embedded + fetched_rows[slot_ids[:, feature]]
    row_count = embedded.shape[0]
    length = lengths[0]
    first_pos = lax.axis_index("ctx") * row_count
    positions = first_pos + jnp.arange(row_count, dtype=jnp.int32)
    valid_rows = positions < length
    score_scale = HEAD ** (-0.5)
    hidden_full = w_out.shape[0]
    normal_x, input_inverse = normalize(embedded)
    normed_input = normal_x.astype(jnp.bfloat16)
    cotangent = grad_out[0]
    masked_g = jnp.where(valid_rows[:, None], cotangent, jnp.zeros_like(cotangent))

    def allowed(query_pos, key_pos):
        return ((key_pos[None, :] <= query_pos[:, None]) & (key_pos[None, :] < length)).astype(
            jnp.float32
        )

    def key_terms(query_block, grad_block, key_block, value_block, query_pos, key_pos):
        key_total = key_block.shape[0]
        block_width = key_block.shape[1]
        scaled = scores(query_block, key_block)
        allowed_mask = allowed(query_pos, key_pos)
        weights = (jax.nn.silu(scaled) * allowed_mask).astype(jnp.bfloat16)
        grad_v = jnp.einsum(
            "hij,ihd->jhd", weights, split_heads(grad_block), preferred_element_type=jnp.float32
        )
        grad_weights = jnp.einsum(
            "ihd,jhd->hij",
            split_heads(grad_block),
            split_heads(value_block),
            preferred_element_type=jnp.float32,
        )
        grad_scores = (grad_weights * silu_slope(scaled) * score_scale * allowed_mask).astype(
            jnp.bfloat16
        )
        grad_k = jnp.einsum(
            "hij,ihd->jhd",
            grad_scores,
            split_heads(query_block),
            preferred_element_type=jnp.float32,
        )
        grad_q = jnp.einsum(
            "hij,jhd->ihd", grad_scores, split_heads(key_block), preferred_element_type=jnp.float32
        )
        return (
            grad_q.reshape(query_block.shape[0], block_width),
            grad_k.reshape(key_total, block_width),
            grad_v.reshape(key_total, block_width),
        )

    head_total = hidden_full // HEAD
    share = head_total // lax.axis_size("ctx")
    head_start = lax.axis_index("ctx") * share
    proj_cols = lax.dynamic_slice_in_dim(
        w_proj.reshape(row_width, 4, head_total, HEAD), head_start, share, 2
    ).reshape(row_width, 4 * share * HEAD)
    out_rows = lax.dynamic_slice_in_dim(
        w_out.reshape(head_total, HEAD, row_width), head_start, share, 0
    ).reshape(share * HEAD, row_width)
    inputs_all, cotangent_all = (
        lax.all_gather(normed_input, "ctx", axis=0, tiled=True),
        lax.all_gather(cotangent, "ctx", axis=0, tiled=True),
    )
    all_total = inputs_all.shape[0]
    all_pos = jnp.arange(all_total, dtype=jnp.int32)
    all_valid = all_pos < length
    pre_mine = jnp.dot(inputs_all, proj_cols, preferred_element_type=jnp.float32)
    act_mine = jax.nn.silu(pre_mine).astype(jnp.bfloat16)
    gating_m, values_m, queries_m, keys_m = jnp.split(act_mine, 4, axis=1)
    width_mine = values_m.shape[1]

    def attend_all(current, subset, first_row):
        key_block, value_block = subset
        key_pos = first_row + jnp.arange(key_block.shape[0], dtype=jnp.int32)
        weights = (jax.nn.silu(scores(queries_m, key_block)) * allowed(all_pos, key_pos)).astype(
            jnp.bfloat16
        )
        summed = jnp.einsum(
            "hij,jhd->ihd", weights, split_heads(value_block), preferred_element_type=jnp.float32
        )
        return current + summed.reshape(all_total, width_mine)

    attended_m = blockwise(
        attend_all, jnp.zeros((all_total, width_mine), jnp.float32), (keys_m, values_m), 0
    )
    row_sum, row_squares = lax.psum(
        (jnp.sum(attended_m, axis=1), jnp.sum(attended_m * attended_m, axis=1)), "ctx"
    )
    middle = (row_sum / hidden_full)[:, None]
    out_inverse = lax.rsqrt((row_squares / hidden_full)[:, None] - middle * middle + epsilon)
    normed_m = (attended_m - middle) * out_inverse
    gated_m = (normed_m * gating_m.astype(jnp.float32)).astype(jnp.bfloat16)
    mixed_rows = lax.psum_scatter(
        jnp.dot(gated_m, out_rows, preferred_element_type=jnp.float32).astype(jnp.bfloat16),
        "ctx",
        scatter_dimension=0,
        tiled=True,
    ).astype(jnp.float32)
    layer_out = jnp.where(valid_rows[:, None], embedded + mixed_rows, 0.0).astype(jnp.bfloat16)
    masked_all = jnp.where(all_valid[:, None], cotangent_all, jnp.zeros_like(cotangent_all))
    grad_gated_m = jnp.einsum("td,hd->th", masked_all, out_rows, preferred_element_type=jnp.float32)
    grad_gating_m = grad_gated_m * normed_m
    t_rows = grad_gated_m * gating_m.astype(jnp.float32)
    t_sum, tn_sum = lax.psum((jnp.sum(t_rows, axis=1), jnp.sum(t_rows * normed_m, axis=1)), "ctx")
    grad_att_m = (
        (t_rows - (t_sum / hidden_full)[:, None] - normed_m * (tn_sum / hidden_full)[:, None])
        * out_inverse
    ).astype(jnp.bfloat16)

    def back_block(step_index, carried):
        first_row = step_index * block_rows
        key_block = lax.dynamic_slice_in_dim(keys_m, first_row, block_rows, 0)
        value_block = lax.dynamic_slice_in_dim(values_m, first_row, block_rows, 0)
        key_pos = first_row + jnp.arange(block_rows, dtype=jnp.int32)
        more_q, more_k, more_v = key_terms(
            queries_m, grad_att_m, key_block, value_block, all_pos, key_pos
        )
        return (
            carried[0] + more_q,
            lax.dynamic_update_slice_in_dim(carried[1], more_k, first_row, 0),
            lax.dynamic_update_slice_in_dim(carried[2], more_v, first_row, 0),
        )

    zero_all = jnp.zeros((all_total, width_mine), jnp.float32)
    grad_q_m, grad_k_m, grad_v_m = lax.fori_loop(
        0, all_total // block_rows, back_block, (zero_all, zero_all, zero_all)
    )
    grad_act_m = jnp.concatenate([grad_gating_m, grad_v_m, grad_q_m, grad_k_m], axis=1)
    grad_pre_m = (grad_act_m * silu_slope(pre_mine)).astype(jnp.bfloat16)
    grad_x = lax.psum_scatter(
        jnp.einsum("tp,dp->td", grad_pre_m, proj_cols, preferred_element_type=jnp.float32).astype(
            jnp.bfloat16
        ),
        "ctx",
        scatter_dimension=0,
        tiled=True,
    ).astype(jnp.float32)
    grad_emb = masked_g.astype(jnp.float32) + norm_back(grad_x, normal_x, input_inverse)
    spread = jnp.broadcast_to(
        grad_emb[:, None, :], (row_count, slot_ids.shape[1], row_width)
    ).reshape(-1, row_width)
    slot_grads = jax.ops.segment_sum(
        spread, slot_ids.reshape(-1), num_segments=fetched_rows.shape[0]
    )
    returned = lax.all_to_all(
        slot_grads.reshape(fetched.shape).astype(jnp.bfloat16),
        "table",
        split_axis=0,
        concat_axis=0,
        tiled=True,
    ).astype(jnp.float32)
    owner_grads = jax.ops.segment_sum(
        returned.reshape(-1, row_width), serve_rows.reshape(-1), num_segments=item_table.shape[0]
    )
    grad_table = lax.psum_scatter(
        owner_grads.astype(jnp.bfloat16), "ctx", scatter_dimension=0, tiled=True
    ).astype(jnp.float32)
    return (layer_out[None], grad_table)


def solution(mesh):
    placed = (
        P("table", None),
        P("table", "ctx"),
        P("table", "ctx", None),
        P("table"),
        P(),
        P(),
        P("table", "ctx", None),
    )
    return jax.shard_map(
        on_device,
        mesh=mesh,
        in_specs=placed,
        out_specs=(P("table", "ctx", None), P(("table", "ctx"), None)),
        check_vma=False,
    )
```

profile of v0, /device:TPU:0, one launch (start us, length us, event | category | flops | bytes accessed | tf_op | source)
XLA Modules:
  0.0 507.3 jit_solution(6258726801934168337)
XLA Ops:
  8.8 16.2 %gather_fusion = f32[4096,256]{1,0:T(8,128)} fusion(f32[2048,256]{1,0:T(8,128)S(1)} %copy-done, s32[4096]{0:T(1024)S(1)} %broadcast_clamp_fusion), kind=kCustom, calls=%fused_computation | custom fusion | bytes 8404992 | tf_op jit(solution)/shard_map/gather | solution.py:58
  25.0 8.5 %all-to-all-start = ((f32[16,256,256]{2,1,0:T(8,128)}), f32[16,256,256]{2,1,0:T(8,128)}, u32[]{:S(2)}, u32[]{:S(2)}) async-start(f32[16,256,256]{2,1,0:T(8,128)} %bitcast.183), calls=%async_computation | async-start | bytes 8388608 | tf_op jit(solution)/shard_map/all_to_all | solution.py:59
  33.7 79.6 %all-to-all-done = f32[16,256,256]{2,1,0:T(8,128)} async-done(((f32[16,256,256]{2,1,0:T(8,128)}), f32[16,256,256]{2,1,0:T(8,128)}, u32[]{:S(2)}, u32[]{:S(2)}) %all-to-all-start) | async-done | bytes 4194336 | tf_op jit(solution)/shard_map/all_to_all | solution.py:59
  113.3 5.6 %gather_fusion.4 = f32[1024,256]{1,0:T(8,128)S(1)} fusion(f32[4096,256]{1,0:T(8,128)} %bitcast.2, s32[1024]{0:T(1024)S(1)} %broadcast_clamp_fusion.1), kind=kCustom, calls=%fused_computation.4 | custom fusion | bytes 2101248 | tf_op jit(solution)/shard_map/gather | solution.py:64
  118.9 5.6 %gather_fusion.3 = f32[1024,256]{1,0:T(8,128)S(1)} fusion(f32[4096,256]{1,0:T(8,128)} %bitcast.2, s32[1024]{0:T(1024)S(1)} %broadcast_clamp_fusion.2), kind=kCustom, calls=%fused_computation.3 | custom fusion | bytes 2101248 | tf_op jit(solution)/shard_map/gather | solution.py:64
  124.6 5.6 %gather_fusion.2 = f32[1024,256]{1,0:T(8,128)S(1)} fusion(f32[4096,256]{1,0:T(8,128)} %bitcast.2, s32[1024]{0:T(1024)S(1)} %broadcast_clamp_fusion.3), kind=kCustom, calls=%fused_computation.2 | custom fusion | bytes 2101248 | tf_op jit(solution)/shard_map/gather | solution.py:64
  130.2 6.9 %gather_fusion.1 = f32[1024,256]{1,0:T(8,128)} fusion(f32[4096,256]{1,0:T(8,128)} %bitcast.2, s32[1024]{0:T(1024)S(1)} %broadcast_clamp_fusion.4), kind=kCustom, calls=%fused_computation.1 | custom fusion | bytes 2101248 | tf_op jit(solution)/shard_map/gather | solution.py:62
  147.4 17.6 %all-gather.4.cloned.1.call-done = bf16[2048,256]{1,0:T(8,128)(2,1)} async-done(((bf16[1024,256]{1,0:T(8,128)(2,1)}), bf16[2048,256]{1,0:T(8,128)(2,1)}) %all-gather.4.cloned.1.call-update) | async-done | bytes 1048592 | tf_op jit(solution)/shard_map/all_gather | solution.py:125
  165.0 5.9 %multiply_convert_fusion = (bf16[2048,1024]{0,1:T(8,128)(2,1)S(1)}, f32[2048,1024]{0,1:T(8,128)}) fusion(bf16[2048,256]{1,0:T(8,128)(2,1)} %all-gather.4.cloned.1.call-done, bf16[256,1024]{1,0:T(8,128)(2,1)S(1)} %reshape.258), kind=kOutput, calls=%fused_computation.58 | convolution fusion | flops 1084227584 | bytes 14155776 | tf_op jit(solution)/shard_map/dot_general | solution.py:131
  175.8 60.2 %while.32 = (s32[]{:T(128)}, f32[2048,256]{0,1:T(8,128)S(1)}, bf16[2048,256]{0,1:T(8,128)(2,1)}, bf16[2048,256]{0,1:T(8,128)(2,1)}, bf16[2048,256]{1,0:T(8,128)(...) while((s32[]{:T(128)}, f32[2048,256]{0,1:T(8,128)S(1)}, ...), condition=%wide.region_3.4_spmd.clone, body=%wide.region_2.3_spmd.clone.sunk | while | flops 1092617728 | bytes 19403956 | solution.py:40
  180.9 7.6 %fusion.117 = f32[2,128,2048]{2,1,0:T(8,128)} fusion(bf16[512,2,128]{0,2,1:T(8,128)(2,1)} %bitcast.187, bf16[512,2,128]{0,2,1:T(8,128)(2,1)S(1)} %bitcast.186, f32[2048,512]{0,1:T(8,128)} %fusion.116, bf16[2048,256]{1,0:T(8,128)(2,1)} %get-tuple-element.574), kind=kOutput, calls=%fused_computation.20.clone.1 | convolution fusion | flops 1088421888 | bytes 7864320 | tf_op jit(solution)/shard_map/while/body/eval_jaxpr/hij,jhd->ihd/dot_general | solution.py:142
  196.0 7.6 %fusion.117 = f32[2,128,2048]{2,1,0:T(8,128)} fusion(bf16[512,2,128]{0,2,1:T(8,128)(2,1)} %bitcast.187, bf16[512,2,128]{0,2,1:T(8,128)(2,1)S(1)} %bitcast.186, f32[2048,512]{0,1:T(8,128)} %fusion.116, bf16[2048,256]{1,0:T(8,128)(2,1)} %get-tuple-element.574), kind=kOutput, calls=%fused_computation.20.clone.1 | convolution fusion | flops 1088421888 | bytes 7864320 | tf_op jit(solution)/shard_map/while/body/eval_jaxpr/hij,jhd->ihd/dot_general | solution.py:142
  211.1 7.6 %fusion.117 = f32[2,128,2048]{2,1,0:T(8,128)} fusion(bf16[512,2,128]{0,2,1:T(8,128)(2,1)} %bitcast.187, bf16[512,2,128]{0,2,1:T(8,128)(2,1)S(1)} %bitcast.186, f32[2048,512]{0,1:T(8,128)} %fusion.116, bf16[2048,256]{1,0:T(8,128)(2,1)} %get-tuple-element.574), kind=kOutput, calls=%fused_computation.20.clone.1 | convolution fusion | flops 1088421888 | bytes 7864320 | tf_op jit(solution)/shard_map/while/body/eval_jaxpr/hij,jhd->ihd/dot_general | solution.py:142
  226.1 7.6 %fusion.117 = f32[2,128,2048]{2,1,0:T(8,128)} fusion(bf16[512,2,128]{0,2,1:T(8,128)(2,1)} %bitcast.187, bf16[512,2,128]{0,2,1:T(8,128)(2,1)S(1)} %bitcast.186, f32[2048,512]{0,1:T(8,128)} %fusion.116, bf16[2048,256]{1,0:T(8,128)(2,1)} %get-tuple-element.574), kind=kOutput, calls=%fused_computation.20.clone.1 | convolution fusion | flops 1088421888 | bytes 7864320 | tf_op jit(solution)/shard_map/while/body/eval_jaxpr/hij,jhd->ihd/dot_general | solution.py:142
  246.8 4.2 fusion.46
  254.3 85.7 %while.33 = (s32[]{:T(128)}, f32[2048,256]{0,1:T(8,128)}, f32[2048,256]{0,1:T(8,128)}, f32[2048,256]{0,1:T(8,128)}, bf16[2048,256]{0,1:T(8,128)(2,1)}, /*index=5...) while((s32[]{:T(128)}, f32[2048,256]{0,1:T(8,128)}, ...), condition=%wide.region_14.15_spmd.clone, body=%wide.region_13.14_spmd.clone.sunk | while | flops 2729444864 | bytes 88874768 | solution.py:189
  261.8 4.5 fusion.133
  283.2 4.5 fusion.133
  287.7 4.0 fusion.130
  304.7 4.5 fusion.133
  309.1 4.0 fusion.130
  326.1 4.5 fusion.133
  330.6 4.0 fusion.130
  340.0 8.9 %fusion.40 = bf16[2048,256]{1,0:T(8,128)(2,1)} fusion(bf16[256,1024]{1,0:T(8,128)(2,1)} %copy-done.12, f32[2048,256]{0,1:T(8,128)} %get-tuple-element.300, f32[2048,256]{0,1:T(8,128)} %get-tuple-element.299, f32[2048,256]{0,1:T(8,128)} %get-tuple-element.298, f32[2048,256]{0,1:T(8,128)} %get-tuple-element.432, f32[2048,1024]{0,1:T(8,128)} %get-tuple-element.446), kind=kOutput, calls=%fused_computation.65 | convolution fusion | flops 1099431936 | bytes 18350080 | tf_op jit(solution)/shard_map/tp,dp->td/dot_general | solution.py:195
  352.7 6.0 %reduce-scatter.6.cloned.1.call-done = bf16[1024,256]{1,0:T(8,128)(2,1)} async-done(((bf16[2048,256]{1,0:T(8,128)(2,1)}), bf16[1024,256]{1,0:T(8,128)(2,1)}) %reduce-scatter.6.cloned.1.call-update) | async-done | bytes 524304 | tf_op jit(solution)/shard_map/reduce_scatter | solution.py:194
  360.6 9.9 %reduce-scatter.4.cloned.1.call-done = bf16[1024,256]{1,0:T(8,128)(2,1)} async-done(((bf16[2048,256]{1,0:T(8,128)(2,1)}), bf16[1024,256]{1,0:T(8,128)(2,1)}) %reduce-scatter.4.cloned.1.call-update) | async-done | bytes 524304 | tf_op jit(solution)/shard_map/reduce_scatter | solution.py:157
  376.0 5.3 %reshape.310 = f32[4096,256]{1,0:T(8,128)} reshape(f32[1024,4,256]{2,1,0:T(4,128)} %broadcast_in_dim.91) | data formatting | bytes 8388608 | tf_op jit(solution)/shard_map/reshape | solution.py:205
  381.3 25.0 %scatter_custom_fusion = f32[4096,256]{1,0:T(8,128)} fusion(s32[4096]{0:T(1024)S(1)} %reshape.308, f32[4096,256]{1,0:T(8,128)} %reshape.310, f32[]{:T(128)} %constant.120.clone.1), kind=kCustom, calls=%fused_computation.70 | custom fusion | flops 1048576 | bytes 4194816 | tf_op jit(solution)/shard_map/scatter-add | solution.py:206
  410.1 6.9 %all-to-all-start.1 = ((bf16[16,256,256]{2,1,0:T(8,128)(2,1)}), bf16[16,256,256]{2,1,0:T(8,128)(2,1)}, u32[]{:S(2)}, u32[]{:S(2)}) async-start(bf16[16,256,256]{2,1,0:T(8,128)(2,1)} %bitcast.13), calls=%async_computation.3 | async-start | bytes 4194304 | tf_op jit(solution)/shard_map/all_to_all | solution.py:209
  417.1 43.2 %all-to-all-done.1 = bf16[16,256,256]{2,1,0:T(8,128)(2,1)} async-done(((bf16[16,256,256]{2,1,0:T(8,128)(2,1)}), bf16[16,256,256]{2,1,0:T(8,128)(2,1)}, u32[]{:S(2)}, u32[]{:S(2)}) %all-to-all-start.1) | async-done | bytes 2097184 | tf_op jit(solution)/shard_map/all_to_all | solution.py:209
  460.3 22.4 %scatter_custom_fusion.1 = f32[2048,256]{1,0:T(8,128)} fusion(s32[4096]{0:T(1024)S(1)} %bitcast.196, bf16[4096,256]{1,0:T(8,128)(2,1)} %bitcast.32, f32[]{:T(128)} %constant.120.clone.1), kind=kCustom, calls=%fused_computation.60 | custom fusion | flops 2097152 | bytes 4194308 | tf_op jit(solution)/shard_map/scatter-add | solution.py:216
  485.4 13.3 %reduce-scatter.8.cloned.1.call-done = bf16[1024,256]{1,0:T(8,128)(2,1)} async-done(((bf16[2048,256]{1,0:T(8,128)(2,1)}), bf16[1024,256]{1,0:T(8,128)(2,1)}) %reduce-scatter.8.cloned.1.call-update) | async-done | bytes 524304 | tf_op jit(solution)/shard_map/reduce_scatter | solution.py:219
  (181 shorter events, 134.9 us)
Async XLA Ops:
  7.2 1.6 copy-start
  25.0 8.6 %copy-start.21 = (s32[1,1024,4]{1,2,0:T(4,128)S(1)}, s32[1,1024,4]{1,2,0:T(4,128)}, u32[]{:S(2)}) copy-start(s32[1,1024,4]{1,2,0:T(4,128)} %param.13) | copy-start | bytes 49156
  25.0 88.3 %all-to-all-start = ((f32[16,256,256]{2,1,0:T(8,128)}), f32[16,256,256]{2,1,0:T(8,128)}, u32[]{:S(2)}, u32[]{:S(2)}) async-start(f32[16,256,256]{2,1,0:T(8,128)} %bitcast.183), calls=%async_computation | async-start | bytes 8388608 | tf_op jit(solution)/shard_map/all_to_all | solution.py:59
  33.5 131.5 %all-gather.4.cloned.1.call-start = ((), (), s32[]{:S(2)}) async-start(), calls=%async_computation.5 | async-start | bytes 1572864 | tf_op jit(solution)/shard_map/all_gather | solution.py:125
  138.6 6.0 %copy-start.23 = (bf16[512,256]{1,0:T(8,128)(2,1)S(1)}, bf16[512,256]{1,0:T(8,128)(2,1)}, u32[]{:S(2)}) copy-start(bf16[512,256]{1,0:T(8,128)(2,1)} %param.16) | copy-start | bytes 786436
  141.3 98.4 %all-gather.6.cloned.1.call-start = ((), (), s32[]{:S(2)}) async-start(), calls=%async_computation.9 | async-start | bytes 1572864 | tf_op jit(solution)/shard_map/all_gather | solution.py:126
  142.1 216.7 %reduce-scatter.6.cloned.1.call-start = ((), (), s32[]{:S(2)}) async-start(), calls=%async_computation.7 | async-start | bytes 1572864 | tf_op jit(solution)/shard_map/reduce_scatter | solution.py:194
  144.6 95.1 %copy-start.9 = (bf16[2,128,256]{2,1,0:T(8,128)(2,1)}, bf16[2,128,256]{2,1,0:T(8,128)(2,1)S(1)}, u32[]{:S(2)}) copy-start(bf16[2,128,256]{2,1,0:T(8,128)(2,1)S(1)} %constant_dynamic-slice_fusion.4) | copy-start | bytes 393220
  147.4 23.5 %copy-start.12 = (bf16[256,1024]{1,0:T(8,128)(2,1)}, bf16[256,1024]{1,0:T(8,128)(2,1)S(1)}, u32[]{:S(2)}) copy-start(bf16[256,1024]{1,0:T(8,128)(2,1)S(1)} %reshape.258) | copy-start | bytes 1572868
  170.9 2.0 copy-start.8
  236.1 10.8 %copy-start.2 = (f32[2048,256]{0,1:T(8,128)}, f32[2048,256]{0,1:T(8,128)S(1)}, u32[]{:S(2)}) copy-start(f32[2048,256]{0,1:T(8,128)S(1)} %get-tuple-element.297) | copy-start | bytes 6291460
  239.7 11.4 %copy-start.13 = (f32[2048]{0:T(1024)}, f32[2048]{0:T(1024)S(1)}, u32[]{:S(2)}) copy-start(f32[2048]{0:T(1024)S(1)} %get-tuple-element.443) | copy-start | bytes 24580
  239.7 11.4 %copy-start.15 = (f32[2048]{0:T(1024)}, f32[2048]{0:T(1024)S(1)}, u32[]{:S(2)}) copy-start(f32[2048]{0:T(1024)S(1)} %get-tuple-element.444) | copy-start | bytes 24580
  251.1 3.2 copy-start.11
  274.0 1.7 copy-start.5
  295.4 1.7 copy-start.5
  314.6 1.6 copy-start.4
  316.8 1.8 copy-start.5
  338.3 1.7 copy-start.5
  340.0 9.3 %copy-start.3 = (f32[2048,256]{0,1:T(8,128)S(1)}, f32[2048,256]{0,1:T(8,128)}, u32[]{:S(2)}) copy-start(f32[2048,256]{0,1:T(8,128)} %copy-done.2) | copy-start | bytes 6291460
  340.0 9.3 %copy-start.10 = (bf16[2,128,256]{2,1,0:T(8,128)(2,1)S(1)}, bf16[2,128,256]{2,1,0:T(8,128)(2,1)}, u32[]{:S(2)}) copy-start(bf16[2,128,256]{2,1,0:T(8,128)(2,1)} %copy-done.9) | copy-start | bytes 393220
  340.0 9.3 %copy-start.14 = (f32[2048]{0:T(1024)S(1)}, f32[2048]{0:T(1024)}, u32[]{:S(2)}) copy-start(f32[2048]{0:T(1024)} %copy-done.13) | copy-start | bytes 24580
  340.0 9.3 %copy-start.16 = (f32[2048]{0:T(1024)S(1)}, f32[2048]{0:T(1024)}, u32[]{:S(2)}) copy-start(f32[2048]{0:T(1024)} %copy-done.15) | copy-start | bytes 24580
  349.0 3.2 copy-start.22
  349.0 9.8 %copy-start.7 = (f32[1024,256]{1,0:T(8,128)S(1)}, f32[1024,256]{1,0:T(8,128)}, u32[]{:S(2)}) copy-start(f32[1024,256]{1,0:T(8,128)} %copy-done.6) | copy-start | bytes 3145732
  349.0 9.8 %copy-start.18 = (f32[1024]{0:T(1024)S(1)}, f32[1024]{0:T(1024)}, u32[]{:S(2)}) copy-start(f32[1024]{0:T(1024)} %copy-done.17) | copy-start | bytes 12292
  349.0 9.8 %copy-start.20 = (f32[1024]{0:T(1024)S(1)}, f32[1024]{0:T(1024)}, u32[]{:S(2)}) copy-start(f32[1024]{0:T(1024)} %copy-done.19) | copy-start | bytes 12292
  349.0 21.5 %reduce-scatter.4.cloned.1.call-start = ((), (), s32[]{:S(2)}) async-start(), calls=%async_computation.6 | async-start | bytes 1572864 | tf_op jit(solution)/shard_map/reduce_scatter | solution.py:157
  406.4 10.7 %copy-start.24 = (s32[16,256]{1,0:T(8,128)S(1)}, s32[16,256]{1,0:T(8,128)}, u32[]{:S(2)}) copy-start(s32[16,256]{1,0:T(8,128)} %param.12) | copy-start | bytes 49156
  410.1 50.2 %all-to-all-start.1 = ((bf16[16,256,256]{2,1,0:T(8,128)(2,1)}), bf16[16,256,256]{2,1,0:T(8,128)(2,1)}, u32[]{:S(2)}, u32[]{:S(2)}) async-start(bf16[16,256,256]{2,1,0:T(8,128)(2,1)} %bitcast.13), calls=%async_computation.3 | async-start | bytes 4194304 | tf_op jit(solution)/shard_map/all_to_all | solution.py:209
  417.0 81.7 %reduce-scatter.8.cloned.1.call-start = ((), (), s32[]{:S(2)}) async-start(), calls=%async_computation.8 | async-start | bytes 1572864 | tf_op jit(solution)/shard_map/reduce_scatter | solution.py:219
  460.3 40.4 %copy-start.1 = (f32[2048,256]{1,0:T(8,128)S(1)}, f32[2048,256]{1,0:T(8,128)}, u32[]{:S(2)}) copy-start(f32[2048,256]{1,0:T(8,128)} %param.11) | copy-start | bytes 6291460
  (6 other events, 7.3 us)
Sparse Core Ops, SparseCore 0:
  141.4 23.5 all-gather.3
  166.5 10.1 all-gather.5
  349.1 9.5 reduce-scatter.5
  360.8 9.5 reduce-scatter.3
  485.5 13.0 reduce-scatter.7
where the time goes:
time: 509 us; the launch traced here: 507 us
  waiting for transfers between devices  170 us (33%)
  other arithmetic  111 us (22%)
  matrix products  99.8 us (20%)
  local copies, waits for them, and re-layouts  88.1 us (17%)
  starting transfers between devices  15.8 us (3%)
  between operations  14.8 us (3%)
  blocking collectives  6.74 us (1%)
    all_to_all x1, waiting for transfers between devices, on_device(): lax.all_to_all(served, 'table', split_axis=0, concat_axis=0, tiled=True)  79.6 us
    all_to_all x1, waiting for transfers between devices, on_device(): lax.all_to_all(slot_grads.reshape(fetched.shape).astype(jnp.bfloat16), 't...  43.2 us
    dot_general x4, matrix products, attend_all(): jnp.einsum('hij,jhd->ihd', weights, split_heads(value_block), preferred_e...  30.4 us
    scatter-add x1, other arithmetic, on_device(): jax.ops.segment_sum(spread, slot_ids.reshape(-1), num_segments=fetched_ro...  25 us
    scatter-add x1, other arithmetic, on_device(): jax.ops.segment_sum(returned.reshape(-1, row_width), serve_rows.reshape(-...  22.4 us
    convert_element_type x8, other arithmetic, allowed(): ((key_pos[None, :] <= query_pos[:, None]) & (key_pos[None, :] < length))....  21.5 us
    dot_general x4, matrix products, key_terms(): jnp.einsum('hij,ihd->jhd', weights, split_heads(grad_block), preferred_el...  17.8 us
    all_gather x1, waiting for transfers between devices, on_device(): lax.all_gather(normed_input, 'ctx', axis=0, tiled=True)  17.6 us
  transfers between devices with their start and end apart: 7, of which 6 were waited for; matrix products, arithmetic and copies ran while one was open for 16% of the time, Pallas kernels for 0%

commit v1 on v0

--- a/solution.py
+++ b/solution.py
@@ -6,6 +6,28 @@
 HEAD = 128
 epsilon = 1e-05
 block_rows = 512
+
+
+def cut_along(array, dim, length):
+    before, after = (array.shape[:dim], array.shape[dim + 1 :])
+    return jnp.moveaxis(array.reshape(*before, length, -1, *after), dim, 0)
+
+
+def in_order(pieces, dim):
+    shape = list(pieces.shape[1:])
+    shape[dim] *= pieces.shape[0]
+    return jnp.moveaxis(pieces, 0, dim).reshape(shape)
+
+
+def swapped_with_each(shard, axis, split_dim, concat_dim):
+    size, index = (lax.axis_size(axis), lax.axis_index(axis))
+    parts = cut_along(shard, split_dim, size)
+    finished = [parts[index]]
+    for step in range(1, size):
+        sent = parts[index ^ step]
+        finished.append(lax.ppermute(sent, axis, [(i, i ^ step) for i in range(size)]))
+    parts = jnp.stack(finished)[index ^ jnp.arange(size)]
+    return in_order(parts, concat_dim)
 
 
 def silu_slope(inputs):
@@ -56,7 +78,7 @@
 def on_device(item_table, serve_rows, token_slots, lengths, w_proj, w_out, grad_out):
     row_width = item_table.shape[1]
     served = item_table[serve_rows]
-    fetched = lax.all_to_all(served, "table", split_axis=0, concat_axis=0, tiled=True)
+    fetched = swapped_with_each(served, "table", 0, 0)
     fetched_rows = fetched.reshape(-1, row_width)
     slot_ids = token_slots[0]
     embedded = fetched_rows[slot_ids[:, 0]]

time: 509 us -> 550 us (1.081)
  waiting for transfers between devices: 170 us -> 139 us
  local copies, waits for them, and re-layouts: 88.1 us -> 113 us
  starting transfers between devices: 15.8 us -> 37.7 us
  matrix products: 99.8 us -> 111 us
  other arithmetic: 111 us -> 120 us
    all_to_all x1 -> x0, waiting for transfers between devices: 79.6 us -> none  [on_device(): lax.all_to_all(served, 'table', split_axis=0, concat_axis=0, tiled=True)]
    ppermute x0 -> x15, waiting for transfers between devices: none -> 63 us  [swapped_with_each(): lax.ppermute(sent, axis, [(i, i ^ step) for i in range(size)])]
    ppermute x0 -> x15, starting transfers between devices: none -> 30 us  [swapped_with_each(): lax.ppermute(sent, axis, [(i, i ^ step) for i in range(size)])]
    unnamed x50 -> x63, local copies, waits for them, and re-layouts: 5.48 us -> 19.9 us
    all_gather x1, waiting for transfers between devices: 17.6 us -> 3.21 us  [on_device(): lax.all_gather(normed_input, 'ctx', axis=0, tiled=True)]
    all_to_all x1 -> x0, starting transfers between devices: 8.52 us -> none  [on_device(): lax.all_to_all(served, 'table', split_axis=0, concat_axis=0, tiled=True)]
    dot_general x4, matrix products: 15.9 us -> 24.2 us  [key_terms(): jnp.einsum('ihd,jhd->hij', split_heads(grad_block), split_heads(value_blo...]
    mul x4, other arithmetic: 3.65 us -> 11.5 us  [key_terms(): grad_weights * silu_slope(scaled) * score_scale * allowed_mask]
  transfers between devices with their start and end apart: 7 -> 21, of which waited for: 6 -> 15; matrix products, arithmetic and copies ran while one was open for 16% -> 17% of each run, Pallas kernels for 0% -> 0%
where the time goes in v1:
time: 550 us; the launch traced here: 544 us
  waiting for transfers between devices  139 us (25%)
  other arithmetic  120 us (22%)
  local copies, waits for them, and re-layouts  113 us (21%)
  matrix products  111 us (20%)
  starting transfers between devices  37.7 us (7%)
  between operations  15.2 us (3%)
  blocking collectives  6.75 us (1%)
    ppermute x15, waiting for transfers between devices, swapped_with_each(): lax.ppermute(sent, axis, [(i, i ^ step) for i in range(size)])  63 us
    all_to_all x1, waiting for transfers between devices, on_device(): lax.all_to_all(slot_grads.reshape(fetched.shape).astype(jnp.bfloat16), 't...  43.2 us
    dot_general x4, matrix products, attend_all(): jnp.einsum('hij,jhd->ihd', weights, split_heads(value_block), preferred_e...  30.5 us
    ppermute x15, starting transfers between devices, swapped_with_each(): lax.ppermute(sent, axis, [(i, i ^ step) for i in range(size)])  30 us
    scatter-add x1, other arithmetic, on_device(): jax.ops.segment_sum(spread, slot_ids.reshape(-1), num_segments=fetched_ro...  25.1 us
    dot_general x4, matrix products, key_terms(): jnp.einsum('ihd,jhd->hij', split_heads(grad_block), split_heads(value_blo...  24.2 us
    scatter-add x1, other arithmetic, on_device(): jax.ops.segment_sum(returned.reshape(-1, row_width), serve_rows.reshape(-...  22.4 us
    convert_element_type x8, other arithmetic, allowed(): ((key_pos[None, :] <= query_pos[:, None]) & (key_pos[None, :] < length))....  21.7 us
  transfers between devices with their start and end apart: 21, of which 15 were waited for; matrix products, arithmetic and copies ran while one was open for 17% of the time, Pallas kernels for 0%

profile of v1, /device:TPU:0, one launch (start us, length us, event | category | flops | bytes accessed | tf_op | source)
XLA Modules:
  0.0 544.2 jit_solution(10672008128205693015)
XLA Ops:
  8.8 16.2 %gather_fusion = f32[4096,256]{1,0:T(8,128)} fusion(f32[2048,256]{1,0:T(8,128)S(1)} %copy-done, s32[4096]{0:T(1024)S(1)} %broadcast_clamp_fusion), kind=kCustom, calls=%fused_computation | custom fusion | bytes 8404992 | tf_op jit(solution)/shard_map/gather | solution.py:80
  28.2 7.0 %collective-permute-start.14 = (f32[1,256,256]{2,1,0:T(8,128)S(1)}, f32[1,256,256]{2,1,0:T(8,128)}, u32[]{:S(2)}, u32[]{:S(2)}) collective-permute-start(f32[1,256,256]{2,1,0:T(8,128)S(1)} %get-tuple-element.437), channel_id=1, source_target_pairs={{0,30},{2,28},{4,26},{6,24},{8,22},{10,20},{12,18},{14,16},{16,14}... | collective-permute-start | bytes 786440 | tf_op jit(solution)/shard_map/ppermute | solution.py:28
  43.7 9.6 %collective-permute-done = f32[1,256,256]{2,1,0:T(8,128)} collective-permute-done((f32[1,256,256]{2,1,0:T(8,128)}, f32[1,256,256]{2,1,0:T(8,128)}, u32[]{:S(2)}, u32[]{:S(2)}) %collective-permute-start) | collective-permute-done | bytes 262176 | tf_op jit(solution)/shard_map/ppermute | solution.py:28
  81.7 5.7 %collective-permute-start.8 = (f32[1,256,256]{2,1,0:T(8,128)S(1)}, f32[1,256,256]{2,1,0:T(8,128)S(1)}, u32[]{:S(2)}, u32[]{:S(2)}) collective-permute-start(f32[1,256,256]{2,1,0:T(8,128)S(1)} %get-tuple-element.443), channel_id=1, source_target_pairs={{0,18},{2,16},{4,22},{6,20},{8,26},{10,24},{12,30},{14,28},{16,2},... | collective-permute-start | bytes 786440 | tf_op jit(solution)/shard_map/ppermute | solution.py:28
  88.2 11.2 %collective-permute-done.7 = f32[1,256,256]{2,1,0:T(8,128)S(1)} collective-permute-done((f32[1,256,256]{2,1,0:T(8,128)S(1)}, f32[1,256,256]{2,1,0:T(8,128)S(1)}, u32[]{:S(2)}, u32[]{:S(2)}) %collective-permute-start.7) | collective-permute-done | bytes 262176 | tf_op jit(solution)/shard_map/ppermute | solution.py:28
  100.1 13.1 %collective-permute-done.8 = f32[1,256,256]{2,1,0:T(8,128)S(1)} collective-permute-done((f32[1,256,256]{2,1,0:T(8,128)S(1)}, f32[1,256,256]{2,1,0:T(8,128)S(1)}, u32[]{:S(2)}, u32[]{:S(2)}) %collective-permute-start.8) | collective-permute-done | bytes 262176 | tf_op jit(solution)/shard_map/ppermute | solution.py:28
  114.0 10.6 %collective-permute-done.9 = f32[1,256,256]{2,1,0:T(8,128)S(1)} collective-permute-done((f32[1,256,256]{2,1,0:T(8,128)S(1)}, f32[1,256,256]{2,1,0:T(8,128)S(1)}, u32[]{:S(2)}, u32[]{:S(2)}) %collective-permute-start.9) | collective-permute-done | bytes 262176 | tf_op jit(solution)/shard_map/ppermute | solution.py:28
  143.6 5.6 %gather_fusion.5 = f32[1024,256]{1,0:T(8,128)S(1)} fusion(f32[4096,256]{1,0:T(8,128)} %bitcast.213, s32[1024]{0:T(1024)S(1)} %get-tuple-element.463), kind=kCustom, calls=%fused_computation.5 | custom fusion | bytes 2101248 | tf_op jit(solution)/shard_map/gather | solution.py:86
  149.3 5.6 %gather_fusion.4 = f32[1024,256]{1,0:T(8,128)S(1)} fusion(f32[4096,256]{1,0:T(8,128)} %bitcast.214, s32[1024]{0:T(1024)S(1)} %get-tuple-element.464), kind=kCustom, calls=%fused_computation.4 | custom fusion | bytes 2101248 | tf_op jit(solution)/shard_map/gather | solution.py:86
  154.9 6.9 %gather_fusion.3 = f32[1024,256]{1,0:T(8,128)} fusion(f32[4096,256]{1,0:T(8,128)} %bitcast.215, s32[1024]{0:T(1024)S(1)} %get-tuple-element.465), kind=kCustom, calls=%fused_computation.3 | custom fusion | bytes 2101248 | tf_op jit(solution)/shard_map/gather | solution.py:86
  161.8 6.9 %gather_fusion.2 = f32[1024,256]{1,0:T(8,128)} fusion(f32[4096,256]{1,0:T(8,128)} %bitcast.216, s32[1024]{0:T(1024)S(1)} %get-tuple-element.466), kind=kCustom, calls=%fused_computation.2 | custom fusion | bytes 2101248 | tf_op jit(solution)/shard_map/gather | solution.py:84
  181.9 5.9 %multiply_convert_fusion = (bf16[2048,1024]{0,1:T(8,128)(2,1)S(1)}, f32[2048,1024]{0,1:T(8,128)}) fusion(bf16[2048,256]{1,0:T(8,128)(2,1)} %all-gather.4.cloned.1.call-done, bf16[256,1024]{1,0:T(8,128)(2,1)S(1)} %reshape.302), kind=kOutput, calls=%fused_computation.59 | convolution fusion | flops 1084227584 | bytes 14155776 | tf_op jit(solution)/shard_map/dot_general | solution.py:153
  192.7 60.4 %while.32 = (s32[]{:T(128)}, f32[2048,256]{0,1:T(8,128)S(1)}, bf16[2048,256]{0,1:T(8,128)(2,1)}, bf16[2048,256]{0,1:T(8,128)(2,1)}, bf16[2048,256]{1,0:T(8,128)(...) while((s32[]{:T(128)}, f32[2048,256]{0,1:T(8,128)S(1)}, ...), condition=%wide.region_3.4_spmd.clone, body=%wide.region_2.3_spmd.clone.sunk | while | flops 1092617728 | bytes 19403956 | solution.py:62
  197.9 7.6 %fusion.118 = f32[2,128,2048]{2,1,0:T(8,128)} fusion(bf16[512,2,128]{0,2,1:T(8,128)(2,1)} %bitcast.227, bf16[512,2,128]{0,2,1:T(8,128)(2,1)S(1)} %bitcast.226, f32[2048,512]{0,1:T(8,128)} %fusion.117, bf16[2048,256]{1,0:T(8,128)(2,1)} %get-tuple-element.591), kind=kOutput, calls=%fused_computation.21.clone.1 | convolution fusion | flops 1088421888 | bytes 7864320 | tf_op jit(solution)/shard_map/while/body/eval_jaxpr/hij,jhd->ihd/dot_general | solution.py:164
  213.0 7.6 %fusion.118 = f32[2,128,2048]{2,1,0:T(8,128)} fusion(bf16[512,2,128]{0,2,1:T(8,128)(2,1)} %bitcast.227, bf16[512,2,128]{0,2,1:T(8,128)(2,1)S(1)} %bitcast.226, f32[2048,512]{0,1:T(8,128)} %fusion.117, bf16[2048,256]{1,0:T(8,128)(2,1)} %get-tuple-element.591), kind=kOutput, calls=%fused_computation.21.clone.1 | convolution fusion | flops 1088421888 | bytes 7864320 | tf_op jit(solution)/shard_map/while/body/eval_jaxpr/hij,jhd->ihd/dot_general | solution.py:164
  228.1 7.6 %fusion.118 = f32[2,128,2048]{2,1,0:T(8,128)} fusion(bf16[512,2,128]{0,2,1:T(8,128)(2,1)} %bitcast.227, bf16[512,2,128]{0,2,1:T(8,128)(2,1)S(1)} %bitcast.226, f32[2048,512]{0,1:T(8,128)} %fusion.117, bf16[2048,256]{1,0:T(8,128)(2,1)} %get-tuple-element.591), kind=kOutput, calls=%fused_computation.21.clone.1 | convolution fusion | flops 1088421888 | bytes 7864320 | tf_op jit(solution)/shard_map/while/body/eval_jaxpr/hij,jhd->ihd/dot_general | solution.py:164
  243.2 7.6 %fusion.118 = f32[2,128,2048]{2,1,0:T(8,128)} fusion(bf16[512,2,128]{0,2,1:T(8,128)(2,1)} %bitcast.227, bf16[512,2,128]{0,2,1:T(8,128)(2,1)S(1)} %bitcast.226, f32[2048,512]{0,1:T(8,128)} %fusion.117, bf16[2048,256]{1,0:T(8,128)(2,1)} %get-tuple-element.591), kind=kOutput, calls=%fused_computation.21.clone.1 | convolution fusion | flops 1088421888 | bytes 7864320 | tf_op jit(solution)/shard_map/while/body/eval_jaxpr/hij,jhd->ihd/dot_general | solution.py:164
  271.5 105.3 %while.33 = (s32[]{:T(128)}, f32[2048,256]{0,1:T(8,128)}, f32[2048,256]{0,1:T(8,128)}, f32[2048,256]{0,1:T(8,128)}, bf16[2048,256]{0,1:T(8,128)(2,1)}, /*index=5...) while((s32[]{:T(128)}, f32[2048,256]{0,1:T(8,128)}, ...), condition=%wide.region_14.15_spmd.clone, body=%wide.region_13.14_spmd.clone.sunk | while | flops 2729444864 | bytes 88874768 | solution.py:211
  286.4 6.0 %fusion.131 = bf16[2,2048,512]{1,2,0:T(8,128)(2,1)S(1)} fusion(f32[2,512,2048]{2,1,0:T(8,128)S(1)} %fusion.129, bf16[512,2,128]{0,2,1:T(8,128)(2,1)S(1)} %bitcast.225, bf16[2048,2,128]{0,2,1:T(8,128)(2,1)} %bitcast.208, f32[2048,512]{0,1:T(8,128)} %fusion.130), kind=kOutput, calls=%fused_computation.40.clone.1 | convolution fusion | flops 559939584 | bytes 18087936 | tf_op jit(solution)/shard_map/while/body/eval_jaxpr/ihd,jhd->hij/dot_general | solution.py:113
  312.7 6.0 %fusion.131 = bf16[2,2048,512]{1,2,0:T(8,128)(2,1)S(1)} fusion(f32[2,512,2048]{2,1,0:T(8,128)S(1)} %fusion.129, bf16[512,2,128]{0,2,1:T(8,128)(2,1)S(1)} %bitcast.225, bf16[2048,2,128]{0,2,1:T(8,128)(2,1)} %bitcast.208, f32[2048,512]{0,1:T(8,128)} %fusion.130), kind=kOutput, calls=%fused_computation.40.clone.1 | convolution fusion | flops 559939584 | bytes 18087936 | tf_op jit(solution)/shard_map/while/body/eval_jaxpr/ihd,jhd->hij/dot_general | solution.py:113
  333.7 5.3 fusion.134
  339.0 6.1 %fusion.131 = bf16[2,2048,512]{1,2,0:T(8,128)(2,1)S(1)} fusion(f32[2,512,2048]{2,1,0:T(8,128)S(1)} %fusion.129, bf16[512,2,128]{0,2,1:T(8,128)(2,1)S(1)} %bitcast.225, bf16[2048,2,128]{0,2,1:T(8,128)(2,1)} %bitcast.208, f32[2048,512]{0,1:T(8,128)} %fusion.130), kind=kOutput, calls=%fused_computation.40.clone.1 | convolution fusion | flops 559939584 | bytes 18087936 | tf_op jit(solution)/shard_map/while/body/eval_jaxpr/ihd,jhd->hij/dot_general | solution.py:113
  365.3 6.0 %fusion.131 = bf16[2,2048,512]{1,2,0:T(8,128)(2,1)S(1)} fusion(f32[2,512,2048]{2,1,0:T(8,128)S(1)} %fusion.129, bf16[512,2,128]{0,2,1:T(8,128)(2,1)S(1)} %bitcast.225, bf16[2048,2,128]{0,2,1:T(8,128)(2,1)} %bitcast.208, f32[2048,512]{0,1:T(8,128)} %fusion.130), kind=kOutput, calls=%fused_computation.40.clone.1 | convolution fusion | flops 559939584 | bytes 18087936 | tf_op jit(solution)/shard_map/while/body/eval_jaxpr/ihd,jhd->hij/dot_general | solution.py:113
  376.8 8.9 %fusion.40 = bf16[2048,256]{1,0:T(8,128)(2,1)} fusion(bf16[256,1024]{1,0:T(8,128)(2,1)} %copy-done.11, f32[2048,256]{0,1:T(8,128)} %get-tuple-element.300, f32[2048,256]{0,1:T(8,128)} %get-tuple-element.299, f32[2048,256]{0,1:T(8,128)} %get-tuple-element.298, f32[2048,256]{0,1:T(8,128)} %get-tuple-element.432, f32[2048,1024]{0,1:T(8,128)} %get-tuple-element.461), kind=kOutput, calls=%fused_computation.66 | convolution fusion | flops 1099431936 | bytes 18350080 | tf_op jit(solution)/shard_map/tp,dp->td/dot_general | solution.py:217
  389.5 6.0 %reduce-scatter.6.cloned.1.call-done = bf16[1024,256]{1,0:T(8,128)(2,1)} async-done(((bf16[2048,256]{1,0:T(8,128)(2,1)}), bf16[1024,256]{1,0:T(8,128)(2,1)}) %reduce-scatter.6.cloned.1.call-update) | async-done | bytes 524304 | tf_op jit(solution)/shard_map/reduce_scatter | solution.py:216
  397.3 9.9 %reduce-scatter.4.cloned.1.call-done = bf16[1024,256]{1,0:T(8,128)(2,1)} async-done(((bf16[2048,256]{1,0:T(8,128)(2,1)}), bf16[1024,256]{1,0:T(8,128)(2,1)}) %reduce-scatter.4.cloned.1.call-update) | async-done | bytes 524304 | tf_op jit(solution)/shard_map/reduce_scatter | solution.py:179
  412.8 5.3 reshape.364
  418.1 25.1 %scatter_custom_fusion = f32[4096,256]{1,0:T(8,128)} fusion(s32[4096]{0:T(1024)S(1)} %reshape.362, f32[4096,256]{1,0:T(8,128)} %reshape.364, f32[]{:T(128)} %constant.156.clone.1), kind=kCustom, calls=%fused_computation.71 | custom fusion | flops 1048576 | bytes 4194816 | tf_op jit(solution)/shard_map/scatter-add | solution.py:228
  446.9 6.9 %all-to-all-start = ((bf16[16,256,256]{2,1,0:T(8,128)(2,1)}), bf16[16,256,256]{2,1,0:T(8,128)(2,1)}, u32[]{:S(2)}, u32[]{:S(2)}) async-start(bf16[16,256,256]{2,1,0:T(8,128)(2,1)} %bitcast.31), calls=%async_computation.2 | async-start | bytes 4194304 | tf_op jit(solution)/shard_map/all_to_all | solution.py:231
  453.9 43.2 %all-to-all-done = bf16[16,256,256]{2,1,0:T(8,128)(2,1)} async-done(((bf16[16,256,256]{2,1,0:T(8,128)(2,1)}), bf16[16,256,256]{2,1,0:T(8,128)(2,1)}, u32[]{:S(2)}, u32[]{:S(2)}) %all-to-all-start) | async-done | bytes 2097184 | tf_op jit(solution)/shard_map/all_to_all | solution.py:231
  497.1 22.4 %scatter_custom_fusion.1 = f32[2048,256]{1,0:T(8,128)} fusion(s32[4096]{0:T(1024)S(1)} %bitcast.234, bf16[4096,256]{1,0:T(8,128)(2,1)} %bitcast.50, f32[]{:T(128)} %constant.156.clone.1), kind=kCustom, calls=%fused_computation.61 | custom fusion | flops 2097152 | bytes 4194308 | tf_op jit(solution)/shard_map/scatter-add | solution.py:238
  522.1 13.3 %reduce-scatter.8.cloned.1.call-done = bf16[1024,256]{1,0:T(8,128)(2,1)} async-done(((bf16[2048,256]{1,0:T(8,128)(2,1)}), bf16[1024,256]{1,0:T(8,128)(2,1)}) %reduce-scatter.8.cloned.1.call-update) | async-done | bytes 524304 | tf_op jit(solution)/shard_map/reduce_scatter | solution.py:241
  (226 shorter events, 223.1 us)
Async XLA Ops:
  7.2 174.7 %all-gather.4.cloned.1.call-start = ((), (), s32[]{:S(2)}) async-start(), calls=%async_computation.4 | async-start | bytes 1572864 | tf_op jit(solution)/shard_map/all_gather | solution.py:147
  24.9 17.0 %copy-start.20 = (s32[1,1024,4]{1,2,0:T(4,128)S(1)}, s32[1,1024,4]{1,2,0:T(4,128)}, u32[]{:S(2)}) copy-start(s32[1,1024,4]{1,2,0:T(4,128)} %param.13) | copy-start | bytes 49156
  28.2 108.7 %collective-permute-start.14 = (f32[1,256,256]{2,1,0:T(8,128)S(1)}, f32[1,256,256]{2,1,0:T(8,128)}, u32[]{:S(2)}, u32[]{:S(2)}) collective-permute-start(f32[1,256,256]{2,1,0:T(8,128)S(1)} %get-tuple-element.437), channel_id=1, source_target_pairs={{0,30},{2,28},{4,26},{6,24},{8,22},{10,20},{12,18},{14,16},{16,14}... | collective-permute-start | bytes 786440 | tf_op jit(solution)/shard_map/ppermute | solution.py:28
  35.2 100.1 %collective-permute-start.13 = (f32[1,256,256]{2,1,0:T(8,128)S(1)}, f32[1,256,256]{2,1,0:T(8,128)}, u32[]{:S(2)}, u32[]{:S(2)}) collective-permute-start(f32[1,256,256]{2,1,0:T(8,128)S(1)} %get-tuple-element.438), channel_id=1, source_target_pairs={{0,28},{2,30},{4,24},{6,26},{8,20},{10,22},{12,16},{14,18},{16,12}... | collective-permute-start | bytes 786440 | tf_op jit(solution)/shard_map/ppermute | solution.py:28
  35.3 98.2 %collective-permute-start.12 = (f32[1,256,256]{2,1,0:T(8,128)S(1)}, f32[1,256,256]{2,1,0:T(8,128)}, u32[]{:S(2)}, u32[]{:S(2)}) collective-permute-start(f32[1,256,256]{2,1,0:T(8,128)S(1)} %get-tuple-element.439), channel_id=1, source_target_pairs={{0,26},{2,24},{4,30},{6,28},{8,18},{10,16},{12,22},{14,20},{16,10}... | collective-permute-start | bytes 786440 | tf_op jit(solution)/shard_map/ppermute | solution.py:28
  38.9 18.3 %collective-permute-start.1 = (f32[1,256,256]{2,1,0:T(8,128)}, f32[1,256,256]{2,1,0:T(8,128)}, u32[]{:S(2)}, u32[]{:S(2)}) collective-permute-start(f32[1,256,256]{2,1,0:T(8,128)} %get-tuple-element.450), channel_id=1, source_target_pairs={{0,4},{2,6},{4,0},{6,2},{8,12},{10,14},{12,8},{14,10},{16,20},{18,... | collective-permute-start | bytes 786440 | tf_op jit(solution)/shard_map/ppermute | solution.py:28
  40.4 12.8 %collective-permute-start = (f32[1,256,256]{2,1,0:T(8,128)}, f32[1,256,256]{2,1,0:T(8,128)}, u32[]{:S(2)}, u32[]{:S(2)}) collective-permute-start(f32[1,256,256]{2,1,0:T(8,128)} %get-tuple-element.451), channel_id=1, source_target_pairs={{0,2},{2,0},{4,6},{6,4},{8,10},{10,8},{12,14},{14,12},{16,18},{18,... | collective-permute-start | bytes 786440 | tf_op jit(solution)/shard_map/ppermute | solution.py:28
  53.3 8.0 %collective-permute-start.2 = (f32[1,256,256]{2,1,0:T(8,128)S(1)}, f32[1,256,256]{2,1,0:T(8,128)S(1)}, u32[]{:S(2)}, u32[]{:S(2)}) collective-permute-start(f32[1,256,256]{2,1,0:T(8,128)S(1)} %get-tuple-element.449), channel_id=1, source_target_pairs={{0,6},{2,4},{4,2},{6,0},{8,14},{10,12},{12,10},{14,8},{16,22},{18,... | collective-permute-start | bytes 786440 | tf_op jit(solution)/shard_map/ppermute | solution.py:28
  57.3 9.2 %collective-permute-start.3 = (f32[1,256,256]{2,1,0:T(8,128)S(1)}, f32[1,256,256]{2,1,0:T(8,128)S(1)}, u32[]{:S(2)}, u32[]{:S(2)}) collective-permute-start(f32[1,256,256]{2,1,0:T(8,128)S(1)} %get-tuple-element.448), channel_id=1, source_target_pairs={{0,8},{2,10},{4,12},{6,14},{8,0},{10,2},{12,4},{14,6},{16,24},{18,... | collective-permute-start | bytes 786440 | tf_op jit(solution)/shard_map/ppermute | solution.py:28
  61.3 10.4 %collective-permute-start.4 = (f32[1,256,256]{2,1,0:T(8,128)S(1)}, f32[1,256,256]{2,1,0:T(8,128)S(1)}, u32[]{:S(2)}, u32[]{:S(2)}) collective-permute-start(f32[1,256,256]{2,1,0:T(8,128)S(1)} %get-tuple-element.447), channel_id=1, source_target_pairs={{0,10},{2,8},{4,14},{6,12},{8,2},{10,0},{12,6},{14,4},{16,26},{18,... | collective-permute-start | bytes 786440 | tf_op jit(solution)/shard_map/ppermute | solution.py:28
  66.4 11.6 %collective-permute-start.5 = (f32[1,256,256]{2,1,0:T(8,128)S(1)}, f32[1,256,256]{2,1,0:T(8,128)S(1)}, u32[]{:S(2)}, u32[]{:S(2)}) collective-permute-start(f32[1,256,256]{2,1,0:T(8,128)S(1)} %get-tuple-element.446), channel_id=1, source_target_pairs={{0,12},{2,14},{4,8},{6,10},{8,4},{10,6},{12,0},{14,2},{16,28},{18,... | collective-permute-start | bytes 786440 | tf_op jit(solution)/shard_map/ppermute | solution.py:28
  71.7 10.1 %collective-permute-start.6 = (f32[1,256,256]{2,1,0:T(8,128)S(1)}, f32[1,256,256]{2,1,0:T(8,128)S(1)}, u32[]{:S(2)}, u32[]{:S(2)}) collective-permute-start(f32[1,256,256]{2,1,0:T(8,128)S(1)} %get-tuple-element.445), channel_id=1, source_target_pairs={{0,14},{2,12},{4,10},{6,8},{8,6},{10,4},{12,2},{14,0},{16,30},{18,... | collective-permute-start | bytes 786440 | tf_op jit(solution)/shard_map/ppermute | solution.py:28
  78.1 21.3 %collective-permute-start.7 = (f32[1,256,256]{2,1,0:T(8,128)S(1)}, f32[1,256,256]{2,1,0:T(8,128)S(1)}, u32[]{:S(2)}, u32[]{:S(2)}) collective-permute-start(f32[1,256,256]{2,1,0:T(8,128)S(1)} %get-tuple-element.444), channel_id=1, source_target_pairs={{0,16},{2,18},{4,20},{6,22},{8,24},{10,26},{12,28},{14,30},{16,0},... | collective-permute-start | bytes 786440 | tf_op jit(solution)/shard_map/ppermute | solution.py:28
  81.7 31.5 %collective-permute-start.8 = (f32[1,256,256]{2,1,0:T(8,128)S(1)}, f32[1,256,256]{2,1,0:T(8,128)S(1)}, u32[]{:S(2)}, u32[]{:S(2)}) collective-permute-start(f32[1,256,256]{2,1,0:T(8,128)S(1)} %get-tuple-element.443), channel_id=1, source_target_pairs={{0,18},{2,16},{4,22},{6,20},{8,26},{10,24},{12,30},{14,28},{16,2},... | collective-permute-start | bytes 786440 | tf_op jit(solution)/shard_map/ppermute | solution.py:28
  99.4 25.2 %collective-permute-start.9 = (f32[1,256,256]{2,1,0:T(8,128)S(1)}, f32[1,256,256]{2,1,0:T(8,128)S(1)}, u32[]{:S(2)}, u32[]{:S(2)}) collective-permute-start(f32[1,256,256]{2,1,0:T(8,128)S(1)} %get-tuple-element.442), channel_id=1, source_target_pairs={{0,20},{2,22},{4,16},{6,18},{8,28},{10,30},{12,24},{14,26},{16,4},... | collective-permute-start | bytes 786440 | tf_op jit(solution)/shard_map/ppermute | solution.py:28
  113.2 18.4 %collective-permute-start.10 = (f32[1,256,256]{2,1,0:T(8,128)S(1)}, f32[1,256,256]{2,1,0:T(8,128)S(1)}, u32[]{:S(2)}, u32[]{:S(2)}) collective-permute-start(f32[1,256,256]{2,1,0:T(8,128)S(1)} %get-tuple-element.441), channel_id=1, source_target_pairs={{0,22},{2,20},{4,18},{6,16},{8,30},{10,28},{12,26},{14,24},{16,6},... | collective-permute-start | bytes 786440 | tf_op jit(solution)/shard_map/ppermute | solution.py:28
  124.6 8.3 %collective-permute-start.11 = (f32[1,256,256]{2,1,0:T(8,128)S(1)}, f32[1,256,256]{2,1,0:T(8,128)S(1)}, u32[]{:S(2)}, u32[]{:S(2)}) collective-permute-start(f32[1,256,256]{2,1,0:T(8,128)S(1)} %get-tuple-element.440), channel_id=1, source_target_pairs={{0,24},{2,26},{4,28},{6,30},{8,16},{10,18},{12,20},{14,22},{16,8},... | collective-permute-start | bytes 786440 | tf_op jit(solution)/shard_map/ppermute | solution.py:28
  172.1 84.8 %all-gather.6.cloned.1.call-start = ((), (), s32[]{:S(2)}) async-start(), calls=%async_computation.8 | async-start | bytes 1572864 | tf_op jit(solution)/shard_map/all_gather | solution.py:148
  172.8 222.7 %reduce-scatter.6.cloned.1.call-start = ((), (), s32[]{:S(2)}) async-start(), calls=%async_computation.6 | async-start | bytes 1572864 | tf_op jit(solution)/shard_map/reduce_scatter | solution.py:216
  175.9 81.0 %copy-start.9 = (bf16[2,128,256]{2,1,0:T(8,128)(2,1)}, bf16[2,128,256]{2,1,0:T(8,128)(2,1)S(1)}, u32[]{:S(2)}) copy-start(bf16[2,128,256]{2,1,0:T(8,128)(2,1)S(1)} %constant_dynamic-slice_fusion.4) | copy-start | bytes 393220
  253.2 10.7 %copy-start.2 = (f32[2048,256]{0,1:T(8,128)}, f32[2048,256]{0,1:T(8,128)S(1)}, u32[]{:S(2)}) copy-start(f32[2048,256]{0,1:T(8,128)S(1)} %get-tuple-element.297) | copy-start | bytes 6291460
  256.8 11.5 %copy-start.12 = (f32[2048]{0:T(1024)}, f32[2048]{0:T(1024)S(1)}, u32[]{:S(2)}) copy-start(f32[2048]{0:T(1024)S(1)} %get-tuple-element.458) | copy-start | bytes 24580
  256.8 11.5 %copy-start.14 = (f32[2048]{0:T(1024)}, f32[2048]{0:T(1024)S(1)}, u32[]{:S(2)}) copy-start(f32[2048]{0:T(1024)S(1)} %get-tuple-element.459) | copy-start | bytes 24580
  376.8 9.3 %copy-start.15 = (f32[2048]{0:T(1024)S(1)}, f32[2048]{0:T(1024)}, u32[]{:S(2)}) copy-start(f32[2048]{0:T(1024)} %copy-done.14) | copy-start | bytes 24580
  385.8 9.8 %copy-start.7 = (f32[1024,256]{1,0:T(8,128)S(1)}, f32[1024,256]{1,0:T(8,128)}, u32[]{:S(2)}) copy-start(f32[1024,256]{1,0:T(8,128)} %copy-done.6) | copy-start | bytes 3145732
  385.8 9.8 %copy-start.17 = (f32[1024]{0:T(1024)S(1)}, f32[1024]{0:T(1024)}, u32[]{:S(2)}) copy-start(f32[1024]{0:T(1024)} %copy-done.16) | copy-start | bytes 12292
  385.8 9.8 %copy-start.19 = (f32[1024]{0:T(1024)S(1)}, f32[1024]{0:T(1024)}, u32[]{:S(2)}) copy-start(f32[1024]{0:T(1024)} %copy-done.18) | copy-start | bytes 12292
  385.8 21.5 %reduce-scatter.4.cloned.1.call-start = ((), (), s32[]{:S(2)}) async-start(), calls=%async_computation.5 | async-start | bytes 1572864 | tf_op jit(solution)/shard_map/reduce_scatter | solution.py:179
  443.2 10.6 %copy-start.23 = (s32[16,256]{1,0:T(8,128)S(1)}, s32[16,256]{1,0:T(8,128)}, u32[]{:S(2)}) copy-start(s32[16,256]{1,0:T(8,128)} %param.12) | copy-start | bytes 49156
  446.9 50.2 %all-to-all-start = ((bf16[16,256,256]{2,1,0:T(8,128)(2,1)}), bf16[16,256,256]{2,1,0:T(8,128)(2,1)}, u32[]{:S(2)}, u32[]{:S(2)}) async-start(bf16[16,256,256]{2,1,0:T(8,128)(2,1)} %bitcast.31), calls=%async_computation.2 | async-start | bytes 4194304 | tf_op jit(solution)/shard_map/all_to_all | solution.py:231
  453.8 81.6 %reduce-scatter.8.cloned.1.call-start = ((), (), s32[]{:S(2)}) async-start(), calls=%async_computation.7 | async-start | bytes 1572864 | tf_op jit(solution)/shard_map/reduce_scatter | solution.py:241
  497.1 40.4 %copy-start.1 = (f32[2048,256]{1,0:T(8,128)S(1)}, f32[2048,256]{1,0:T(8,128)}, u32[]{:S(2)}) copy-start(f32[2048,256]{1,0:T(8,128)} %param.11) | copy-start | bytes 6291460
  (19 other events, 70.4 us)
Sparse Core Ops, SparseCore 0:
  172.2 9.6 all-gather.3
  183.4 10.1 all-gather.5
  385.9 9.5 reduce-scatter.5
  397.6 9.5 reduce-scatter.3
  522.3 13.0 reduce-scatter.7
